TPU v7x, 32 devices: a whole 2x2x4 slice. The times are simulated.
32 devices in a mesh: subj: 2 (over y), band: 4 (over z), lon: 2 (over x), pop: 2 (over core).
Axes of the slice: x: 2, y: 2, z: 4, core: 2. Of those that a mesh axis runs over, the one named last changes fastest.
Arguments:
- activity: float32 [16, 640, 1280], P(('subj', 'pop'), 'band', 'lon'), parts along dimension 0, may hold values from -6 to 6
- drive: bfloat16 [16, 640, 1280], P(('subj', 'pop'), 'band', 'lon'), parts along dimension 0, may hold values from -6 to 6
- basis: bfloat16 [1280, 320, 640], P(('subj', 'band', 'lon')), parts along dimension 0, may hold values from -6 to 6
- kernels: float32 [4, 640], replicated, may hold values from 0.2 to 2
- conn_block: int32 [8, 8], replicated, may hold values from 0 to 3
- coupling: float32 [16, 8], P('subj'), parts along dimension 0, may hold values from -2.5 to 2.5
- rate_params: float32 [8, 8], P('subj'), parts along dimension 0, may hold values from 0.5 to 2
Outputs:
- activity_next: float32 [16, 640, 1280], P(('subj', 'pop'), 'band', 'lon'), parts along dimension 0
There are 2 independent parts, one for each index of `subj`. A program takes and returns all parts, laid end to end along the dimension named above; an argument that names none is the same for every part. Nothing has to cross between parts.
All inputs are finite; a program needn't handle non-finite values.
Results may differ from a plain program's by a relative error of at most 0.0095.
Values may be sent and summed in bfloat16 or wider, within the bound.
A program may use at most 192 MiB of HBM per device.

v0:
```python
import math

import jax
import jax.numpy as jnp
from jax import lax
from jax.sharding import PartitionSpec as P

NLAT = 640
NLON = 1280
DEG = 640
STEPS = 2


time_step = 0.5


def with_halo(shard, sides, width):
    for axis, dim in sides:
        size, length = (lax.axis_size(axis), shard.shape[dim])
        up = [(i, (i + 1) % size) for i in range(size - 1)]
        down = [(j, i) for i, j in up]
        last = lax.slice_in_dim(shard, length - width, length, axis=dim)
        leading = lax.slice_in_dim(shard, 0, width, axis=dim)
        before = lax.ppermute(last, axis, up)
        after = lax.ppermute(leading, axis, down)
        shard = jnp.concatenate([before, shard, after], axis=dim)
    return shard


def fourier_table():
    longitude = jnp.arange(NLON, dtype=jnp.int32)
    wavenumber = jnp.arange(DEG, dtype=jnp.int32)
    phase = longitude[:, None] * wavenumber[None, :] % NLON
    angle = phase.astype(jnp.float32) * (2.0 * math.pi / NLON)
    return jnp.stack([jnp.cos(angle), jnp.sin(angle)], axis=1).astype(jnp.bfloat16)


def lat_weights():
    row_index = jnp.arange(NLAT // 2, dtype=jnp.float32)
    colatitude = math.pi * (4.0 * row_index + 3.0) / (4.0 * NLAT + 2.0)
    return math.pi * jnp.sin(colatitude) / NLAT


def to_owners(fourier):
    return lax.all_to_all(fourier, ("band", "lon"), split_axis=2, concat_axis=3, tiled=True)


def to_latitudes(synthesis):
    return lax.all_to_all(synthesis, ("band", "lon"), split_axis=3, concat_axis=2, tiled=True)


def local(activity, drive, basis, kernels, conn_block, coupling, rate_params):
    pop_here = activity.shape[0]
    owned_count = basis.shape[0]
    half_lat = basis.shape[1]
    quarter = DEG // 2
    owner_index = lax.axis_index("band") * lax.axis_size("lon") + lax.axis_index("lon")
    pop_first = lax.axis_index("pop") * pop_here
    params = lax.dynamic_slice_in_dim(rate_params, pop_first, pop_here, 1)
    gain_row, thresh, decay_row, lateral = (params[0], params[1], params[2], params[3])
    cos_sin = fourier_table()
    weights = lat_weights()
    wavenumber = owner_index * owned_count + jnp.arange(owned_count, dtype=jnp.int32)
    degree = jnp.arange(DEG, dtype=jnp.int32)
    triangle = degree[None, :] >= wavenumber[:, None]
    slots = jnp.arange(2, dtype=jnp.int32)
    parity_pick = (slots[None, :] == (wavenumber % 2)[:, None])[None, None, :, :, None]
    every_wave = jnp.arange(DEG, dtype=jnp.int32)
    amplitude = jnp.where(every_wave == 0, 1.0, 2.0).astype(jnp.bfloat16)
    coup_own = lax.dynamic_slice_in_dim(coupling, pop_first, pop_here, 0)
    block_own = lax.dynamic_slice_in_dim(conn_block, pop_first, pop_here, 0)
    onehot = (block_own[..., None] == jnp.arange(kernels.shape[0], dtype=jnp.int32)).astype(
        jnp.float32
    )
    mixing = coup_own[..., None] * jnp.einsum(
        "ijb,bn->ijn", onehot, kernels, precision=lax.Precision.HIGHEST
    )
    basis_split = basis.reshape(owned_count, half_lat, quarter, 2)
    drive_f32 = drive.astype(jnp.float32)
    activity_now = activity
    for step_index in range(STEPS):
        rates = jax.nn.sigmoid(
            gain_row[:, None, None] * (activity_now - thresh[:, None, None])
        ).astype(jnp.bfloat16)
        lat_rows = lax.all_to_all(rates, "lon", split_axis=1, concat_axis=2, tiled=True)
        fourier = jnp.einsum(
            "ijk,kcm->icmj", lat_rows, cos_sin, preferred_element_type=jnp.float32
        ).astype(jnp.bfloat16)
        spectrum = to_owners(fourier)
        northern = spectrum[..., :half_lat].astype(jnp.float32)
        southern = jnp.flip(spectrum[..., half_lat:], axis=3).astype(jnp.float32)
        even_part = (weights * (northern + southern)).astype(jnp.bfloat16)
        odd_part = (weights * (northern - southern)).astype(jnp.bfloat16)
        operand = jnp.where(parity_pick, even_part[:, :, :, None, :], odd_part[:, :, :, None, :])
        coeffs = jnp.einsum(
            "icmsj,mjqs->icmqs", operand, basis_split, preferred_element_type=jnp.float32
        )
        coeffs = coeffs.reshape(pop_here, 2, owned_count, DEG)
        coeffs = jnp.where(triangle[None, None], coeffs, 0.0)
        gathered = lax.all_gather(coeffs.astype(jnp.bfloat16), "pop", axis=0, tiled=True).astype(
            coeffs.dtype
        )
        mixed_spec = jnp.sum(mixing[:, :, None, None, :] * gathered[None], axis=1).astype(
            jnp.bfloat16
        )
        degree_parts = jnp.einsum(
            "icmqs,mjqs->icmsj",
            mixed_spec.reshape(pop_here, 2, owned_count, quarter, 2),
            basis_split,
            preferred_element_type=jnp.float32,
        )
        same_parity = jnp.sum(jnp.where(parity_pick, degree_parts, 0.0), axis=3)
        other_parity = jnp.sum(jnp.where(parity_pick, 0.0, degree_parts), axis=3)
        synthesis = jnp.concatenate(
            [same_parity + other_parity, jnp.flip(same_parity - other_parity, axis=3)], axis=3
        ).astype(jnp.bfloat16)
        returned = to_latitudes(synthesis)
        scaled = returned * amplitude[None, None, :, None]
        synth_field = jnp.einsum(
            "icmj,kcm->ijk", scaled, cos_sin, preferred_element_type=jnp.float32
        ) * (1.0 / NLON)
        padded = with_halo(lat_rows, ((("band", "lon"), 1),), 1).astype(jnp.float32)
        rates_f32 = lat_rows.astype(jnp.float32)
        lateral_term = (
            jnp.roll(rates_f32, 1, axis=2)
            + jnp.roll(rates_f32, -1, axis=2)
            + padded[:, 2:, :]
            + padded[:, :-2, :]
            - 4.0 * rates_f32
        )
        coupled = synth_field + lateral[:, None, None] * lateral_term
        coupled_grid = lax.all_to_all(
            coupled.astype(jnp.bfloat16), "lon", split_axis=2, concat_axis=1, tiled=True
        ).astype(coupled.dtype)
        forcing = -decay_row[:, None, None] * activity_now + coupled_grid + drive_f32
        activity_now = activity_now + time_step * forcing
    return activity_now


def solution(mesh):
    in_specs = (
        P(("subj", "pop"), "band", "lon"),
        P(("subj", "pop"), "band", "lon"),
        P(("subj", "band", "lon"), None, None),
        P(),
        P(),
        P("subj", None),
        P("subj", None),
    )
    out_specs = P(("subj", "pop"), "band", "lon")
    return jax.shard_map(local, mesh=mesh, in_specs=in_specs, out_specs=out_specs, check_vma=False)
```

profile of v0, /device:TPU:0, one launch (start us, length us, event | category | flops | bytes accessed | tf_op | source)
XLA Modules:
  0.0 531.6 jit_solution(762499637347597196)
XLA Ops:
  11.7 4.2 all-to-all-start
  15.9 14.5 %sine_convert_fusion = (bf16[1280,1,640]{2,0,1:T(8,128)(2,1)S(1)}, bf16[1280,1,640]{2,0,1:T(8,128)(2,1)}) fusion(), kind=kLoop, calls=%fused_computation.14 | loop fusion | flops 9011200 | bytes 3276800 | tf_op jit(solution)/shard_map/convert.13
  31.9 3.7 fusion.54
  38.9 7.1 %all-to-all-start.1 = ((bf16[4,2,640,80]{3,0,1,2:T(4,128)(2,1)}), bf16[4,2,640,80]{3,0,1,2:T(4,128)(2,1)S(1)}, u32[]{:S(2)}, u32[]{:S(2)}) async-start(bf16[4,2,640,80]{3,0,1,2:T(4,128)(2,1)} %copy.136), calls=%async_computation.1 | async-start | bytes 2621440 | tf_op jit(solution)/shard_map/all_to_all | solution.py:45
  46.4 48.1 %copy.140 = bf16[80,320,640]{1,0,2:T(8,128)(2,1)} copy(bf16[80,320,640]{2,1,0:T(8,128)(2,1)} %param.9) | data formatting | bytes 65536000 | tf_op args[2]
  94.5 53.5 %copy.170 = bf16[80,320,320,2,1]{2,1,4,3,0:T(8,128)(2,1)} copy(bf16[80,320,320,2,1]{1,0,3,2,4:T(8,128)(2,1)} %bitcast.160) | data formatting | bytes 65536000 | tf_op jit(solution)/shard_map/reshape | solution.py:78
  155.7 16.3 %convolution_bitcast_fusion.1 = bf16[4,2,80,320,2]{3,0,1,4,2:T(4,128)(2,1)} fusion(bf16[80,320,320,2,1]{2,1,4,3,0:T(8,128)(2,1)} %copy.170, pred[80,2]{1,0:T(8,128)(4,1)S(1)} %iota_compare_fusion.1, bf16[4,2,80,320]{3,0,1,2:T(4,128)(2,1)S(1)} %copy.139, bf16[4,2,80,320]{3,0,1,2:T(4,128)(2,1)S(1)} %copy.138), kind=kOutput, calls=%fused_computation.55 | convolution fusion | flops 262553600 | bytes 34406560 | tf_op jit(solution)/shard_map/icmsj,mjqs->icmqs/dot_general | solution.py:95
  172.0 4.1 copy.142
  179.3 10.1 %all-gather.3.cloned.1.call-done = bf16[8,2,80,640]{3,2,1,0:T(8,128)(2,1)} async-done(((bf16[4,2,80,640]{3,2,1,0:T(8,128)(2,1)}), bf16[8,2,80,640]{3,2,1,0:T(8,128)(2,1)}) %all-gather.3.cloned.1.call-update) | async-done | bytes 1638416 | tf_op jit(solution)/shard_map/all_gather | solution.py:100
  195.6 18.7 %select_reduce_fusion.2 = (f32[80,4,2,320]{3,1,2,0:T(4,128)S(1)}, f32[80,4,2,320]{3,1,2,0:T(4,128)S(1)}) fusion(pred[80,2]{1,0:T(8,128)(4,1)S(1)} %iota_compare_fusion.1, bf16[4,2,80,320,2]{3,0,1,4,2:T(4,128)(2,1)} %copy.145, bf16[80,320,320,2,1]{2,1,4,3,0:T(8,128)(2,1)} %copy.170), kind=kOutput, calls=%fused_computation.32 | convolution fusion | flops 263372800 | bytes 35225760 | tf_op jit(solution)/shard_map/icmqs,mjqs->icmsj/dot_general | solution.py:106
  215.7 3.5 reverse.1
  223.2 5.8 %all-to-all-start.2 = ((bf16[4,2,80,640]{2,1,0,3:T(2,128)(2,1)}), bf16[4,2,80,640]{2,1,0,3:T(2,128)(2,1)S(1)}, u32[]{:S(2)}, u32[]{:S(2)}) async-start(bf16[4,2,80,640]{2,1,0,3:T(2,128)(2,1)} %copy.147), calls=%async_computation.2 | async-start | bytes 2621440 | tf_op jit(solution)/shard_map/all_to_all | solution.py:49
  229.0 3.9 collective-permute-start
  242.1 18.9 %all-to-all-done.2 = bf16[4,2,80,640]{2,1,0,3:T(2,128)(2,1)S(1)} async-done(((bf16[4,2,80,640]{2,1,0,3:T(2,128)(2,1)}), bf16[4,2,80,640]{2,1,0,3:T(2,128)(2,1)S(1)}, u32[]{:S(2)}, u32[]{:S(2)}) %all-to-all-start.2) | async-done | bytes 819232 | tf_op jit(solution)/shard_map/all_to_all | solution.py:49
  262.9 5.6 %fusion.31 = bf16[4,80,1280]{2,1,0:T(8,128)(2,1)S(1)} fusion(f32[4,82,1280]{2,1,0:T(8,128)} %maximum_convert_fusion, f32[4,80,1279]{2,1,0:T(8,128)} %get-tuple-element.20, f32[4,80,1]{2,1,0:T(8,128)} %get-tuple-element.22, f32[4,80,1]{2,1,0:T(8,128)} %get-tuple-element.21, f32[4,80,1279]{2,1,0:T(8,128)} %get-tuple-element.19, f32[4]{0:T(128)S(1)} %copy-done.16, ...), kind=kOutput, calls=%fused_computation.26 | convolution fusion | flops 1055539200 | bytes 12289296 | tf_op jit(solution)/shard_map/icmj,kcm->ijk/dot_general | solution.py:119
  270.1 19.1 %all_to_all.126 = bf16[4,80,1280]{1,0,2:T(4,128)(2,1)} all-to-all(bf16[4,80,1280]{1,0,2:T(4,128)(2,1)S(1)} %copy.150), channel_id=1, replica_groups=mesh['subj'=2,'band'=4,'lon'=2,'pop'=2] {'lon'}, dimensions={2} | all-to-all | bytes 1638400 | tf_op jit(solution)/shard_map/all_to_all | solution.py:132
  295.1 12.2 %all_to_all.127 = bf16[4,160,640]{2,0,1:T(4,128)(2,1)S(1)} all-to-all(bf16[4,160,640]{2,0,1:T(4,128)(2,1)S(1)} %copy.152), channel_id=1, replica_groups=mesh['subj'=2,'band'=4,'lon'=2,'pop'=2] {'lon'}, dimensions={1} | all-to-all | bytes 1638400 | tf_op jit(solution)/shard_map/all_to_all | solution.py:85
  308.8 4.1 fusion.51
  316.3 36.5 %all_to_all.128 = bf16[4,2,640,80]{3,0,1,2:T(4,128)(2,1)S(1)} all-to-all(bf16[4,2,640,80]{3,0,1,2:T(4,128)(2,1)} %copy.154), channel_id=1, replica_groups=mesh['subj'=2,'band'=4,'lon'=2,'pop'=2] {'band','lon'}, dimensions={2} | all-to-all | bytes 1638400 | tf_op jit(solution)/shard_map/all_to_all | solution.py:45
  357.8 12.1 %reverse.2 = bf16[4,2,80,384]{3,2,1,0:T(8,128)(2,1)} reverse(bf16[4,2,80,384]{3,2,1,0:T(8,128)(2,1)} %bitcast.183), dimensions={3} | reverse | bytes 983040
  372.0 16.3 %convolution_bitcast_fusion = bf16[4,2,80,320,2]{3,0,1,4,2:T(4,128)(2,1)} fusion(bf16[80,320,320,2,1]{2,1,4,3,0:T(8,128)(2,1)} %copy.170, pred[80,2]{1,0:T(8,128)(4,1)S(1)} %iota_compare_fusion.1, bf16[4,2,80,320]{3,0,1,2:T(4,128)(2,1)S(1)} %copy.157, bf16[4,2,80,320]{3,0,1,2:T(4,128)(2,1)S(1)} %copy.156), kind=kOutput, calls=%fused_computation.54 | convolution fusion | flops 262553600 | bytes 34406560 | tf_op jit(solution)/shard_map/icmsj,mjqs->icmqs/dot_general | solution.py:95
  388.3 5.1 copy.159
  396.6 8.5 %all-gather.5.cloned.1.call-done = bf16[8,2,80,640]{3,2,1,0:T(8,128)(2,1)} async-done(((bf16[4,2,80,640]{3,2,1,0:T(8,128)(2,1)}), bf16[8,2,80,640]{3,2,1,0:T(8,128)(2,1)}) %all-gather.5.cloned.1.call-update) | async-done | bytes 1638416 | tf_op jit(solution)/shard_map/all_gather | solution.py:100
  409.1 4.9 copy.162
  414.0 19.4 %select_reduce_fusion = (f32[80,4,2,320]{3,1,2,0:T(4,128)S(1)}, f32[80,4,2,320]{3,1,2,0:T(4,128)}) fusion(pred[80,2]{1,0:T(8,128)(4,1)S(1)} %iota_compare_fusion.1, bf16[4,2,80,320,2]{3,0,1,4,2:T(4,128)(2,1)} %copy.162, bf16[80,320,320,2,1]{2,1,4,3,0:T(8,128)(2,1)} %copy.170), kind=kOutput, calls=%fused_computation.30 | convolution fusion | flops 263372800 | bytes 35225760 | tf_op jit(solution)/shard_map/icmqs,mjqs->icmsj/dot_general | solution.py:106
  445.4 5.8 %all-to-all-start.6 = ((bf16[4,2,80,640]{2,1,0,3:T(2,128)(2,1)}), bf16[4,2,80,640]{2,1,0,3:T(2,128)(2,1)}, u32[]{:S(2)}, u32[]{:S(2)}) async-start(bf16[4,2,80,640]{2,1,0,3:T(2,128)(2,1)} %copy.164), calls=%async_computation.6 | async-start | bytes 2621440 | tf_op jit(solution)/shard_map/all_to_all | solution.py:49
  451.2 3.9 collective-permute-start.2
  464.3 19.0 %all-to-all-done.6 = bf16[4,2,80,640]{2,1,0,3:T(2,128)(2,1)} async-done(((bf16[4,2,80,640]{2,1,0,3:T(2,128)(2,1)}), bf16[4,2,80,640]{2,1,0,3:T(2,128)(2,1)}, u32[]{:S(2)}, u32[]{:S(2)}) %all-to-all-start.6) | async-done | bytes 819232 | tf_op jit(solution)/shard_map/all_to_all | solution.py:49
  488.8 6.5 %fusion.34 = bf16[4,80,1280]{2,1,0:T(8,128)(2,1)} fusion(f32[4,82,1280]{2,1,0:T(8,128)} %maximum_convert_fusion.1, f32[4,80,1279]{2,1,0:T(8,128)} %get-tuple-element.14, f32[4,80,1]{2,1,0:T(8,128)} %get-tuple-element.16, f32[4,80,1]{2,1,0:T(8,128)S(1)} %get-tuple-element.15, f32[4,80,1279]{2,1,0:T(8,128)} %get-tuple-element.13, ...), kind=kOutput, calls=%fused_computation.27 | convolution fusion | flops 1055539200 | bytes 12289296 | tf_op jit(solution)/shard_map/icmj,kcm->ijk/dot_general | solution.py:119
  498.1 19.1 %all_to_all.129 = bf16[4,80,1280]{1,0,2:T(4,128)(2,1)} all-to-all(bf16[4,80,1280]{1,0,2:T(4,128)(2,1)S(1)} %copy.167), channel_id=1, replica_groups=mesh['subj'=2,'band'=4,'lon'=2,'pop'=2] {'lon'}, dimensions={2} | all-to-all | bytes 1638400 | tf_op jit(solution)/shard_map/all_to_all | solution.py:132
  517.1 3.8 copy.168
  520.9 3.6 fusion.40
  (122 shorter events, 99.7 us)
Async XLA Ops:
  6.5 172.0 %copy-start = (f32[4,640]{1,0:T(4,128)S(1)}, f32[4,640]{1,0:T(4,128)}, u32[]{:S(2)}) copy-start(f32[4,640]{1,0:T(4,128)} %param.10) | copy-start | bytes 30724
  7.8 0.6 copy-start.9
  11.7 18.8 %all-to-all-start = ((bf16[4,160,640]{2,0,1:T(4,128)(2,1)}), bf16[4,160,640]{2,0,1:T(4,128)(2,1)S(1)}, u32[]{:S(2)}, u32[]{:S(2)}) async-start(bf16[4,160,640]{2,0,1:T(4,128)(2,1)} %copy.134), calls=%async_computation | async-start | bytes 1638400 | tf_op jit(solution)/shard_map/all_to_all | solution.py:85
  30.5 1.4 copy-start.6
  38.9 109.3 %all-to-all-start.1 = ((bf16[4,2,640,80]{3,0,1,2:T(4,128)(2,1)}), bf16[4,2,640,80]{3,0,1,2:T(4,128)(2,1)S(1)}, u32[]{:S(2)}, u32[]{:S(2)}) async-start(bf16[4,2,640,80]{3,0,1,2:T(4,128)(2,1)} %copy.136), calls=%async_computation.1 | async-start | bytes 2621440 | tf_op jit(solution)/shard_map/all_to_all | solution.py:45
  46.0 143.3 %all-gather.3.cloned.1.call-start = ((), (), s32[]{:S(2)}) async-start(), calls=%async_computation.8 | async-start | bytes 2457600 | tf_op jit(solution)/shard_map/all_gather | solution.py:100
  148.2 28.5 %copy-start.7 = (pred[80,640]{1,0:T(8,128)(4,1)}, pred[80,640]{1,0:T(8,128)(4,1)S(1)}, u32[]{:S(2)}) copy-start(pred[80,640]{1,0:T(8,128)(4,1)S(1)} %iota_compare_fusion) | copy-start | bytes 153604
  176.8 1.7 copy-start.14
  176.8 1.7 copy-start.15
  223.2 37.8 %all-to-all-start.2 = ((bf16[4,2,80,640]{2,1,0,3:T(2,128)(2,1)}), bf16[4,2,80,640]{2,1,0,3:T(2,128)(2,1)S(1)}, u32[]{:S(2)}, u32[]{:S(2)}) async-start(bf16[4,2,80,640]{2,1,0,3:T(2,128)(2,1)} %copy.147), calls=%async_computation.2 | async-start | bytes 2621440 | tf_op jit(solution)/shard_map/all_to_all | solution.py:49
  228.9 176.1 %all-gather.5.cloned.1.call-start = ((), (), s32[]{:S(2)}) async-start(), calls=%async_computation.9 | async-start | bytes 2457600 | tf_op jit(solution)/shard_map/all_gather | solution.py:100
  229.0 11.3 %collective-permute-start = (bf16[4,1,1280]{2,1,0:T(2,128)(2,1)S(1)}, bf16[4,1,1280]{2,1,0:T(2,128)(2,1)S(1)}, u32[]{:S(2)}, u32[]{:S(2)}) collective-permute-start(bf16[4,1,1280]{2,1,0:T(2,128)(2,1)S(1)} %get-tuple-element.23), channel_id=1, source_target_pairs={{0,2},{2,4},{4,6},{6,8},{8,10},{10,12},{12,14},{1,3},{3,5},{5,7},{... | collective-permute-start | bytes 30728 | tf_op jit(solution)/shard_map/ppermute | solution.py:24
  232.9 7.7 %collective-permute-start.1 = (bf16[4,1,1280]{2,1,0:T(2,128)(2,1)S(1)}, bf16[4,1,1280]{2,1,0:T(2,128)(2,1)S(1)}, u32[]{:S(2)}, u32[]{:S(2)}) collective-permute-start(bf16[4,1,1280]{2,1,0:T(2,128)(2,1)S(1)} %get-tuple-element.24), channel_id=1, source_target_pairs={{2,0},{4,2},{6,4},{8,6},{10,8},{12,10},{14,12},{3,1},{5,3},{7,5},{... | collective-permute-start | bytes 30728 | tf_op jit(solution)/shard_map/ppermute | solution.py:25
  261.8 1.0 copy-start.13
  261.9 1.0 copy-start.16
  289.2 3.0 copy-start.2
  289.2 3.0 copy-start.10
  289.2 3.0 copy-start.11
  292.2 2.6 copy-start.3
  393.4 1.6 copy-start.8
  433.4 2.4 copy-start.5
  445.4 37.9 %all-to-all-start.6 = ((bf16[4,2,80,640]{2,1,0,3:T(2,128)(2,1)}), bf16[4,2,80,640]{2,1,0,3:T(2,128)(2,1)}, u32[]{:S(2)}, u32[]{:S(2)}) async-start(bf16[4,2,80,640]{2,1,0,3:T(2,128)(2,1)} %copy.164), calls=%async_computation.6 | async-start | bytes 2621440 | tf_op jit(solution)/shard_map/all_to_all | solution.py:49
  451.2 11.3 %collective-permute-start.2 = (bf16[4,1,1280]{2,1,0:T(2,128)(2,1)S(1)}, bf16[4,1,1280]{2,1,0:T(2,128)(2,1)S(1)}, u32[]{:S(2)}, u32[]{:S(2)}) collective-permute-start(bf16[4,1,1280]{2,1,0:T(2,128)(2,1)S(1)} %get-tuple-element.17), channel_id=1, source_target_pairs={{0,2},{2,4},{4,6},{6,8},{8,10},{10,12},{12,14},{1,3},{3,5},{5,7},{... | collective-permute-start | bytes 30728 | tf_op jit(solution)/shard_map/ppermute | solution.py:24
  455.1 7.7 %collective-permute-start.3 = (bf16[4,1,1280]{2,1,0:T(2,128)(2,1)S(1)}, bf16[4,1,1280]{2,1,0:T(2,128)(2,1)S(1)}, u32[]{:S(2)}, u32[]{:S(2)}) collective-permute-start(bf16[4,1,1280]{2,1,0:T(2,128)(2,1)S(1)} %get-tuple-element.18), channel_id=1, source_target_pairs={{2,0},{4,2},{6,4},{8,6},{10,8},{12,10},{14,12},{3,1},{5,3},{7,5},{... | collective-permute-start | bytes 30728 | tf_op jit(solution)/shard_map/ppermute | solution.py:25
  486.6 2.2 copy-start.17
  517.1 3.8 copy-start.4
  517.1 3.8 copy-start.12
  520.9 3.6 copy-start.1
Sparse Core Ops, SparseCore 0:
  178.0 11.2 all-gather.2
  396.2 8.8 all-gather.4
where the time goes:
time: 541 us; the launch traced here: 532 us
  local copies, waits for them, and re-layouts  199 us (37%)
  matrix products  90.8 us (17%)
  blocking collectives  86.9 us (16%)
  waiting for transfers between devices  63.6 us (12%)
  other arithmetic  43.2 us (8%)
  starting transfers between devices  33.7 us (6%)
  between operations  14.2 us (3%)
    unnamed x43, local copies, waits for them, and re-layouts  70.9 us
    reshape x1, local copies, waits for them, and re-layouts, local(): basis_split = basis.reshape(owned_count, half_lat, quarter, 2)  53.5 us
    all_to_all x2, blocking collectives, local(): lax.all_to_all(coupled.astype(jnp.bfloat16), 'lon', split_axis=2, concat_...  38.1 us
    dot_general x2, matrix products, local(): jnp.einsum('icmqs,mjqs->icmsj', mixed_spec.reshape(pop_here, 2, owned_cou...  38.1 us
    all_to_all x2, waiting for transfers between devices, to_latitudes(): lax.all_to_all(synthesis, ('band', 'lon'), split_axis=3, concat_axis=2, t...  37.9 us
    all_to_all x1, blocking collectives, to_owners(): lax.all_to_all(fourier, ('band', 'lon'), split_axis=2, concat_axis=3, til...  36.5 us
    dot_general x2, matrix products, local(): jnp.einsum('icmsj,mjqs->icmqs', operand, basis_split, preferred_element_t...  32.6 us
    all_gather x2, waiting for transfers between devices, local(): lax.all_gather(coeffs.astype(jnp.bfloat16), 'pop', axis=0, tiled=True)  18.5 us
  transfers between devices with their start and end apart: 10, of which 8 were waited for; matrix products, arithmetic and copies ran while one was open for 24% of the time, Pallas kernels for 0%

commit v1 on v0

--- a/solution.py
+++ b/solution.py
@@ -1,8 +1,11 @@
+import functools
 import math
 
 import jax
 import jax.numpy as jnp
 from jax import lax
+from jax.experimental import pallas as pl
+from jax.experimental.pallas import tpu as pltpu
 from jax.sharding import PartitionSpec as P
 
 NLAT = 640
@@ -137,6 +140,471 @@
     return activity_now
 
 
+MESH = pl.DeviceIdType.MESH
+LANES = 128
+
+
+def remote(src, dst, send_sem, recv_sem, peer):
+    return pltpu.make_async_remote_copy(
+        src_ref=src, dst_ref=dst, send_sem=send_sem, recv_sem=recv_sem,
+        device_id=peer, device_id_type=MESH,
+    )
+
+
+def step_kernel(nband, last, rates_ref, t_ref, mirror_ref, mirrors_ref, w_ref, b_hbm, a_ref, k_ref,
+                u_ref, drive_ref, par_ref, *rest):
+    if last:
+        un_ref, *rest = rest
+    else:
+        un_ref, rn_ref, *rest = rest
+    (face_ref, ps_ref, pr_ref, fz_ref, gz_ref, b_ref, own_ref, other_ref, x_ref, y_ref, s_ref, o_ref,
+     field_ref, pad_ref, edge_ref, around_ref, af_ref, col_ref, side_ref, we_ref,
+     bsem, ps, pr, zs, zr, ss, rs, ys, yr, xs, xr, es, er) = rest
+    band, lon = lax.axis_index("band"), lax.axis_index("lon")
+    rows, nlon = rates_ref.shape
+    owned, half_lat, deg = b_ref.shape
+    groups = t_ref.shape[0]
+    group = owned // groups
+    half = own_ref.shape[1]
+    both = 2 * half
+    npop = half // 2
+    hb = nband // 2
+    nlat = half_lat // hb
+    lines = 2 * group
+    first = (band * lax.axis_size("lon") + lon) * owned
+    kinds = k_ref.shape[0]
+    across = {"lon": 1 - lon}
+    mate = {"pop": 1 - lax.axis_index("pop")}
+    tiles = x_ref.shape[0]
+    spare = tiles * LANES - half_lat
+    padding = [jnp.zeros((group, spare), jnp.float32)] if spare else []
+    wide_padding = [jnp.zeros((both, spare), jnp.float32)] if spare else []
+    degree = lax.broadcasted_iota(jnp.int32, (half, deg), 1)
+    along = (((1,), (1,)), ((), ()))
+    down = (((0,), (0,)), ((), ()))
+
+    def forward_band(d):
+        return lax.rem(band + d, nband)
+
+    def backward_band(d):
+        return lax.rem(band + nband - d, nband)
+
+    def fetch(g):
+        part = pl.ds(g * group, group)
+        return pltpu.make_async_copy(b_hbm.at[part], b_ref.at[part], bsem.at[g])
+
+    def partial(g):
+        return remote(ps_ref.at[g], pr_ref.at[g], ps.at[g], pr.at[g], across)
+
+    def outward(g, d):
+        dest = forward_band(d)
+        return remote(
+            fz_ref.at[g, dest], gz_ref.at[g, band], zs.at[g, d - 1], zr.at[g, d - 1], {"band": dest}
+        )
+
+    def swap(g):
+        part = pl.ds(g * group, group)
+        return remote(own_ref.at[part], other_ref.at[part], ss.at[g], rs.at[g], mate)
+
+    def homeward(g, d):
+        dest = forward_band(d)
+        return remote(
+            s_ref.at[g, dest], o_ref.at[g, 0, band], ys.at[g, d - 1], yr.at[g, d - 1], {"band": dest}
+        )
+
+    def cross(g, d):
+        source = backward_band(d)
+        block = s_ref.at[g, band] if d == 0 else o_ref.at[g, 0, source]
+        return remote(block, o_ref.at[g, 1, source], xs.at[g, d], xr.at[g, d], across)
+
+    def edge(side):
+        peer = {"band": forward_band(1 if side == 0 else nband - 1)}
+        return remote(edge_ref.at[side], around_ref.at[side], es.at[side], er.at[side], peer)
+
+    def column():
+        return remote(col_ref, side_ref, es.at[2], er.at[2], across)
+
+    @pl.loop(0, groups)
+    def _(g):
+        fetch(g).start()
+
+    barrier = pltpu.get_barrier_semaphore()
+    for d in range(1, nband):
+        peer = {"band": forward_band(d)}
+        pl.semaphore_signal(barrier, inc=1, device_id=peer, device_id_type=MESH)
+    pl.semaphore_signal(barrier, inc=1, device_id=across, device_id_type=MESH)
+    pl.semaphore_signal(barrier, inc=1, device_id=mate, device_id_type=MESH)
+
+    for i in range(npop):
+        part = pl.ds(i * nlat, nlat)
+        face_ref[part] = jnp.dot(
+            mirror_ref[...], rates_ref[part], preferred_element_type=jnp.float32
+        ).astype(face_ref.dtype)
+    fill = jnp.zeros((16 - npop, nlon), jnp.float32)
+    for side, at in ((0, nlat - 1), (1, 0)):
+        picked = [
+            rates_ref[i * nlat + at : i * nlat + at + 1].astype(jnp.float32) for i in range(npop)
+        ]
+        edge_ref[side] = jnp.concatenate(picked + [fill], axis=0).astype(edge_ref.dtype)
+    r16 = lax.broadcasted_iota(jnp.int32, (16, nlon), 0)
+    c16 = lax.broadcasted_iota(jnp.int32, (16, nlon), 1)
+    pick = ((r16 == 0) & (c16 == nlon - 1)) | ((r16 == 1) & (c16 == 0))
+    col_ref[...] = lax.dot_general(
+        jnp.where(pick, 1.0, 0.0).astype(jnp.bfloat16), rates_ref[...], along,
+        preferred_element_type=jnp.float32,
+    ).astype(col_ref.dtype)
+    pl.semaphore_wait(barrier, nband + 1)
+
+    @pl.loop(0, groups)
+    def _(g):
+        ps_ref[g] = lax.dot_general(
+            t_ref[g, 1], face_ref[...], along, preferred_element_type=jnp.float32
+        ).astype(ps_ref.dtype)
+        partial(g).start()
+
+    edge(0).start()
+    edge(1).start()
+    column().start()
+    field_ref[...] = jnp.zeros_like(field_ref)
+
+    def analyse_longitudes(g):
+        total = lax.dot_general(
+            t_ref[g, 0], face_ref[...], along, preferred_element_type=jnp.float32
+        )
+        partial(g).wait_recv()
+        total = (total + pr_ref[g].astype(jnp.float32)).astype(fz_ref.dtype)
+        fz_ref[g] = total.reshape(fz_ref.shape[1:])
+        for d in range(1, nband):
+            outward(g, d).start()
+        gz_ref[g, band] = fz_ref[g, band]
+
+    def analyse_latitudes(g):
+        for d in range(1, nband):
+            outward(g, d).wait_recv()
+        for cc in range(2):
+            part = slice(cc * group, (cc + 1) * group)
+            parts = []
+            for h in range(hb):
+                north = gz_ref[g, h, part, :].astype(jnp.float32)
+                south = gz_ref[g, nband - 1 - h, part, :].astype(jnp.float32)
+                parts.append((w_ref[h] * (north + south), w_ref[h] * (north - south)))
+            for side in range(2):
+                for i in range(npop):
+                    row = side * half + i * 2 + cc
+                    line = [piece[side][:, i * nlat : (i + 1) * nlat] for piece in parts]
+                    line = jnp.concatenate(line + padding, axis=1)
+                    for t in range(tiles):
+                        x_ref[t, pl.ds(row, group, stride=both), :] = line[
+                            :, t * LANES : (t + 1) * LANES
+                        ]
+        fetch(g).wait()
+        for k in range(group):
+            m = g * group + k
+            x = [x_ref[t, k * both : (k + 1) * both, :] for t in range(tiles)]
+            x = jnp.concatenate(x, axis=1)[:, :half_lat].astype(jnp.bfloat16)
+            parity = jnp.dot(x, b_ref[m], preferred_element_type=jnp.float32)
+            gap = degree - (first + m)
+            coeffs = jnp.where(gap % 2 == 0, parity[:half], parity[half:])
+            own_ref[m] = jnp.where(gap >= 0, coeffs, 0.0).astype(own_ref.dtype)
+        swap(g).start()
+
+    def synthesise(g):
+        swap(g).wait_recv()
+        for k in range(group):
+            m = g * group + k
+            pair = jnp.concatenate(
+                [own_ref[m].astype(jnp.float32), other_ref[m].astype(jnp.float32)], axis=0
+            ).astype(jnp.bfloat16)
+            by_kind = jnp.dot(
+                a_ref[...], jnp.concatenate([pair, pair], axis=0),
+                preferred_element_type=jnp.float32,
+            )
+            mixed = k_ref[0:1] * by_kind[:half]
+            for kind in range(1, kinds):
+                mixed += k_ref[kind : kind + 1] * by_kind[kind * half : (kind + 1) * half]
+            gap = degree - (first + m)
+            signed = jnp.where(gap % 2 == 0, mixed, -mixed)
+            y = lax.dot_general(
+                jnp.concatenate([mixed, signed], axis=0).astype(jnp.bfloat16), b_ref[m],
+                along, preferred_element_type=jnp.float32,
+            )
+            y = y * jnp.where(first + m == 0, 1.0, 2.0)
+            y = jnp.concatenate([y] + wide_padding, axis=1)
+            for t in range(tiles):
+                y_ref[t, k * both : (k + 1) * both, :] = y[:, t * LANES : (t + 1) * LANES]
+        for side in range(2):
+            blocks = [[None, None] for h in range(hb)]
+            for cc in range(2):
+                wide = [
+                    jnp.concatenate(
+                        [
+                            y_ref[t, pl.ds(side * half + i * 2 + cc, group, stride=both), :]
+                            for t in range(tiles)
+                        ],
+                        axis=1,
+                    )
+                    for i in range(npop)
+                ]
+                for h in range(hb):
+                    blocks[h][cc] = jnp.concatenate(
+                        [row[:, h * nlat : (h + 1) * nlat] for row in wide], axis=1
+                    ).astype(s_ref.dtype)
+            joined = jnp.concatenate([piece for block in blocks for piece in block], axis=0)
+            if side == 1:
+                joined = jnp.dot(
+                    joined, mirrors_ref[...], preferred_element_type=jnp.float32
+                ).astype(s_ref.dtype)
+            for h in range(hb):
+                dest = h if side == 0 else nband - 1 - h
+                s_ref[g, dest] = joined[h * lines : (h + 1) * lines]
+        for d in range(1, nband):
+            homeward(g, d).start()
+        cross(g, 0).start()
+        o_ref[g, 0, band] = s_ref[g, band]
+
+    def pass_on(g):
+        for d in range(1, nband):
+            homeward(g, d).wait_recv()
+            cross(g, d).start()
+
+    def synthesise_longitudes(g):
+        for d in range(nband):
+            cross(g, d).wait_recv()
+        waves = 2 * nband * lines
+        table = t_ref[g].reshape(waves, nlon)
+        for q in range(0, rows, LANES):
+            field_ref[q : q + LANES] += lax.dot_general(
+                o_ref[g, :, :, :, q : q + LANES].reshape(waves, LANES), table, down,
+                preferred_element_type=jnp.float32,
+            )
+
+    stages = (analyse_longitudes, analyse_latitudes, synthesise, pass_on, synthesise_longitudes)
+
+    @pl.loop(0, groups + len(stages) - 1)
+    def _(t):
+        for late, stage in enumerate(stages):
+            @pl.when((t >= late) & (t < groups + late))
+            def _():
+                stage(t - late)
+
+    edge(0).wait_recv()
+    edge(1).wait_recv()
+    column().wait_recv()
+    af_ref[...] = around_ref[...].astype(jnp.float32)
+    r16 = lax.broadcasted_iota(jnp.int32, (16, LANES), 0)
+    c16 = lax.broadcasted_iota(jnp.int32, (16, LANES), 1)
+    place = ((r16 == 0) & (c16 == LANES - 1)) | ((r16 == 1) & (c16 == 0))
+    we_ref[...] = lax.dot_general(
+        side_ref[...], jnp.where(place, 1.0, 0.0).astype(jnp.bfloat16), down,
+        preferred_element_type=jnp.float32,
+    )
+    step = 16
+    scale = 1.0 / (2 * nlon)
+    at = lax.broadcasted_iota(jnp.int32, (step, nlon), 1)
+
+    @pl.loop(0, npop)
+    def _(i):
+        gain, thresh, decay, lateral = (par_ref[k, i] for k in range(4))
+        base = pl.multiple_of(i * nlat, step)
+        pad_ref[pl.ds(8, nlat)] = rates_ref[pl.ds(base, nlat)].astype(jnp.float32)
+        pad_ref[7:8] = jnp.where(band > 0, af_ref[0, pl.ds(i, 1)], 0.0)
+        pad_ref[8 + nlat : 9 + nlat] = jnp.where(band < nband - 1, af_ref[1, pl.ds(i, 1)], 0.0)
+        for r in range(0, nlat, step):
+            here = pl.ds(base + r, step)
+            own = pad_ref[8 + r : 8 + r + step]
+            ends = we_ref[here]
+            beside = (
+                jnp.where(at == 0, ends[:, LANES - 1 :], pltpu.roll(own, 1, 1))
+                + jnp.where(at == nlon - 1, ends[:, :1], pltpu.roll(own, nlon - 1, 1))
+                + pad_ref[9 + r : 9 + r + step]
+                + pad_ref[7 + r : 7 + r + step]
+                - 4.0 * own
+            )
+            u = u_ref[here]
+            forcing = (
+                -decay * u + field_ref[here] * scale + lateral * beside
+                + drive_ref[here].astype(jnp.float32)
+            )
+            u = u + time_step * forcing
+            un_ref[here] = u
+            if not last:
+                rn_ref[here] = jax.nn.sigmoid(gain * (u - thresh)).astype(rn_ref.dtype)
+
+    edge(0).wait_send()
+    edge(1).wait_send()
+    column().wait_send()
+
+    @pl.loop(0, groups)
+    def _(g):
+        partial(g).wait_send()
+        swap(g).wait_send()
+        for d in range(1, nband):
+            outward(g, d).wait_send()
+            homeward(g, d).wait_send()
+        for d in range(nband):
+            cross(g, d).wait_send()
+
+
+def one_step(rates, table, mirror, mirrors, weights, basis, by_kind, kernels, u, drive, params,
+             nband, npop, last):
+    rows, nlon = rates.shape
+    owned, half_lat, deg = basis.shape
+    nlat = rows // npop
+    groups = table.shape[0]
+    group = owned // groups
+    half = 2 * npop
+    tiles = pl.cdiv(half_lat, LANES)
+    dma = pltpu.SemaphoreType.DMA
+    vmem = pl.BlockSpec(memory_space=pltpu.VMEM)
+    hbm = pl.BlockSpec(memory_space=pltpu.MemorySpace.HBM)
+    shapes = [jax.ShapeDtypeStruct(u.shape, jnp.float32)]
+    if not last:
+        shapes.append(jax.ShapeDtypeStruct(rates.shape, jnp.bfloat16))
+    bf16 = jnp.bfloat16
+    blocks = (groups, nband, 2 * group, rows)
+    waves = nband * 2 * group
+    return pl.pallas_call(
+        functools.partial(step_kernel, nband, last),
+        out_shape=tuple(shapes),
+        in_specs=[vmem] * 5 + [hbm] + [vmem] * 4 + [pl.BlockSpec(memory_space=pltpu.SMEM)],
+        out_specs=(vmem,) * len(shapes),
+        scratch_shapes=[
+            pltpu.VMEM((rows, nlon), bf16),
+            pltpu.VMEM((groups, waves, rows), bf16),
+            pltpu.VMEM((groups, waves, rows), bf16),
+            pltpu.VMEM(blocks, bf16),
+            pltpu.VMEM(blocks, bf16),
+            pltpu.VMEM(basis.shape, bf16),
+            pltpu.VMEM((owned, half, deg), bf16),
+            pltpu.VMEM((owned, half, deg), bf16),
+            pltpu.VMEM((tiles, group * 2 * half, LANES), jnp.float32),
+            pltpu.VMEM((tiles, group * 2 * half, LANES), jnp.float32),
+            pltpu.VMEM(blocks, bf16),
+            pltpu.VMEM((groups, 2) + blocks[1:], bf16),
+            pltpu.VMEM((rows, nlon), jnp.float32),
+            pltpu.VMEM((nlat + 16, nlon), jnp.float32),
+            pltpu.VMEM((2, 16, nlon), bf16),
+            pltpu.VMEM((2, 16, nlon), bf16),
+            pltpu.VMEM((2, 16, nlon), jnp.float32),
+            pltpu.VMEM((16, rows), bf16),
+            pltpu.VMEM((16, rows), bf16),
+            pltpu.VMEM((rows, LANES), jnp.float32),
+            dma((groups,)),
+            dma((groups,)), dma((groups,)),
+            dma((groups, nband - 1)), dma((groups, nband - 1)),
+            dma((groups,)), dma((groups,)),
+            dma((groups, nband - 1)), dma((groups, nband - 1)),
+            dma((groups, nband)), dma((groups, nband)),
+            dma((3,)), dma((3,)),
+        ],
+        compiler_params=pltpu.CompilerParams(
+            collective_id=1 if last else 0, has_side_effects=True, vmem_limit_bytes=60 * 2**20
+        ),
+        name="last_step" if last else "one_step",
+    )(rates, table, mirror, mirrors, weights, basis, by_kind, kernels, u, drive, params)
+
+
+def wave_table(starts, owned, longitude, period):
+    coarse = starts[:, None] + 16 * jnp.arange(owned // 16, dtype=jnp.int32)[None, :]
+    fine = jnp.arange(16, dtype=jnp.int32)
+
+    def angles(wave):
+        phase = wave[..., None] * longitude % period
+        angle = phase.astype(jnp.float32) * (2.0 * math.pi / period)
+        return lax.optimization_barrier((jnp.cos(angle), jnp.sin(angle)))
+
+    cos_a, sin_a = (v[:, :, None, :] for v in angles(coarse))
+    cos_b, sin_b = (v[None, None, :, :] for v in angles(fine))
+    shape = (starts.shape[0], owned, longitude.shape[0])
+    cosine = (cos_a * cos_b - sin_a * sin_b).reshape(shape)
+    sine = (sin_a * cos_b + cos_a * sin_b).reshape(shape)
+    return jnp.stack([cosine, sine], axis=1)
+
+
+def fast_local(activity, drive, basis, kernels, conn_block, coupling, rate_params):
+    npop, nlat, nlon = activity.shape
+    owned, half_lat, deg = basis.shape
+    nband = lax.axis_size("band")
+    hb = nband // 2
+    period = nlon * lax.axis_size("lon")
+    rows = npop * nlat
+    band, lon, pop = lax.axis_index("band"), lax.axis_index("lon"), lax.axis_index("pop")
+    pop_first = pop * npop
+    params = lax.dynamic_slice_in_dim(rate_params, pop_first, npop, 1)
+    gain_row, thresh = params[0, :, None, None], params[1, :, None, None]
+
+    bands = jnp.arange(nband, dtype=jnp.int32)
+    kk = jnp.arange(nlon, dtype=jnp.int32)
+    own_start = (bands * 2 + lon) * owned
+    other_start = (bands * 2 + 1 - lon) * owned
+    starts = jnp.concatenate([own_start, other_start])
+    table = wave_table(starts, owned, lon * nlon + kk, period).astype(jnp.bfloat16)
+    table = table.reshape(2, nband, 2, owned // 16, 16, nlon).transpose(3, 0, 1, 2, 4, 5)
+    table = table.reshape(owned // 16, 2, nband * 32, nlon)
+
+    row_index = jnp.arange(half_lat, dtype=jnp.float32)
+    colatitude = math.pi * (4.0 * row_index + 3.0) / (8.0 * half_lat + 2.0)
+    weights = math.pi * jnp.sin(colatitude) / (2.0 * half_lat)
+    weights = jnp.tile(weights.reshape(hb, 1, nlat), (1, 1, npop))
+
+    south = band >= hb
+    lat = jnp.arange(nlat, dtype=jnp.int32)
+    mirror = (lat[:, None] == jnp.where(south, nlat - 1 - lat, lat)[None, :]).astype(jnp.bfloat16)
+    back = (lat[:, None] == nlat - 1 - lat[None, :]).astype(jnp.bfloat16)
+    mirrors = jnp.einsum("xy,ab->xayb", jnp.eye(npop, dtype=jnp.bfloat16), back)
+    mirrors = mirrors.reshape(rows, rows)
+
+    coup_own = lax.dynamic_slice_in_dim(coupling, pop_first, npop, 0)
+    block_own = lax.dynamic_slice_in_dim(conn_block, pop_first, npop, 0)
+    kind = jnp.arange(kernels.shape[0], dtype=jnp.int32)
+    per_kind = jnp.where(block_own[None] == kind[:, None, None], coup_own[None], 0.0)
+    per_kind = jnp.concatenate(
+        [
+            lax.dynamic_slice_in_dim(per_kind, pop_first, npop, 2),
+            lax.dynamic_slice_in_dim(per_kind, (1 - pop) * npop, npop, 2),
+        ],
+        axis=2,
+    )
+    spread = per_kind[:, :, None, :, None] * jnp.eye(2, dtype=jnp.float32)[:, None, :]
+    spread = spread.reshape(kernels.shape[0] * npop * 2, 2 * npop * 2)
+    coarse = lax.reduce_precision(spread, 8, 7)
+    by_kind = jnp.concatenate([coarse, spread - coarse], axis=1).astype(jnp.bfloat16)
+
+    drive = drive.reshape(rows, nlon)
+    u = activity.reshape(rows, nlon)
+    rates = jax.nn.sigmoid(gain_row * (activity - thresh)).astype(jnp.bfloat16)
+    rates = rates.reshape(rows, nlon)
+    for step_index in range(STEPS):
+        last = step_index == STEPS - 1
+        results = one_step(
+            rates, table, mirror, mirrors, weights, basis, by_kind, kernels, u, drive, params,
+            nband, npop, last,
+        )
+        if last:
+            (u,) = results
+        else:
+            u, rates = results
+    return u.reshape(npop, nlat, nlon)
+
+
+def dispatch(activity, drive, basis, *rest):
+    npop, nlat, nlon = activity.shape
+    owned, half_lat, deg = basis.shape
+    fits = (
+        lax.axis_size("lon") == 2
+        and lax.axis_size("pop") == 2
+        and lax.axis_size("band") % 2 == 0
+        and npop == 4
+        and owned % 16 == 0
+        and nlat % 16 == 0
+        and (npop * nlat) % LANES == 0
+        and nlon % LANES == 0
+        and deg % LANES == 0
+        and 2 * basis.size <= 40 * 2**20
+    )
+    return (fast_local if fits else local)(activity, drive, basis, *rest)
+
+
 def solution(mesh):
     in_specs = (
         P(("subj", "pop"), "band", "lon"),
@@ -148,4 +616,6 @@
         P("subj", None),
     )
     out_specs = P(("subj", "pop"), "band", "lon")
-    return jax.shard_map(local, mesh=mesh, in_specs=in_specs, out_specs=out_specs, check_vma=False)
+    return jax.shard_map(
+        dispatch, mesh=mesh, in_specs=in_specs, out_specs=out_specs, check_vma=False
+    )

time: 541 us -> 144 us (0.27); the launches traced: 532 us -> 144 us
  local copies, waits for them, and re-layouts: 199 us -> 7.15 us
  Pallas kernels: 0 us -> 129 us
  matrix products: 90.8 us -> 0 us
  blocking collectives: 86.9 us -> 0 us
  waiting for transfers between devices: 63.6 us -> 0 us
  other arithmetic: 43.2 us -> 7.73 us
  starting transfers between devices: 33.7 us -> 0 us
  between operations: 14.2 us -> 0.11 us
    pallas_call x0 -> x2, Pallas kernels: none -> 129 us  [one_step(): pl.pallas_call(functools.partial(step_kernel, nband, last), out_shape=tup...]
    dot_general x9 -> x0, matrix products: 90.8 us -> none  [the longest x2 38.1 us: local(): jnp.einsum('icmqs,mjqs->icmsj', mixed_spec.reshape(pop_here, 2, owned_cou...]
    all_to_all x4 -> x0, blocking collectives: 86.9 us -> none  [the longest x2 38.1 us: local(): lax.all_to_all(coupled.astype(jnp.bfloat16), 'lon', split_axis=2, concat_...]
    unnamed x43 -> x5, local copies, waits for them, and re-layouts: 70.9 us -> 2.71 us
    reshape x3 -> x1, local copies, waits for them, and re-layouts: 55.8 us -> 1.76 us  [fast_local(): mirrors = mirrors.reshape(rows, rows)]
    all_to_all x4 -> x0, waiting for transfers between devices: 37.9 us -> none  [the longest x2 37.9 us: to_latitudes(): lax.all_to_all(synthesis, ('band', 'lon'), split_axis=3, concat_axis=2, t...]
    convert_element_type x16 -> x0, local copies, waits for them, and re-layouts: 30.7 us -> none  [the longest x4 10.1 us: local(): jnp.sum(mixing[:, :, None, None, :] * gathered[None], axis=1)]
    all_to_all x4 -> x0, starting transfers between devices: 22.9 us -> none  [the longest x2 11.6 us: to_latitudes(): lax.all_to_all(synthesis, ('band', 'lon'), split_axis=3, concat_axis=2, t...]
  transfers between devices with their start and end apart: 10 -> 0, of which waited for: 8 -> 0; matrix products, arithmetic and copies ran while one was open for 24% -> 0% of each run, Pallas kernels for 0% -> 0%
where the time goes in v1:
time: 144 us
  Pallas kernels  129 us (90%)
  other arithmetic  7.73 us (5%)
  local copies, waits for them, and re-layouts  7.15 us (5%)
    pallas_call x2, Pallas kernels, one_step(): pl.pallas_call(functools.partial(step_kernel, nband, last), out_shape=tup...  129 us

profile of v1, /device:TPU:0, one launch (start us, length us, event | category | flops | bytes accessed | tf_op | source)
XLA Modules:
  0.0 144.2 jit_solution(8534255972371310275)
XLA Ops:
  0.0 0.0 copy-start
  0.0 0.1 pad_add_fusion
  0.1 0.8 constant_dynamic-slice_fusion.4.par_ref
  0.9 0.0 copy-start.1
  0.9 0.0 copy-done
  0.9 0.1 copy.12
  1.0 0.7 constant_dynamic-slice_fusion.2
  1.7 0.1 copy.13
  1.8 0.1 sine_multiply_fusion
  1.8 0.1 broadcast_add_fusion
  1.9 0.7 tile.13.w_ref
  2.6 0.6 fusion.mirror_ref
  3.3 0.2 fusion.13
  3.5 0.1 broadcast_multiply_fusion
  3.6 0.2 mul.225
  3.7 0.1 copy.15
  3.8 0.1 copy.14
  3.9 0.7 pad_maximum_fusion.2.a_ref
  4.6 0.5 fusion.6
  5.2 2.9 %divide_convert_fusion = bf16[4,160,640]{2,1,0:T(8,128)(2,1)} fusion(f32[4,160,640]{2,1,0:T(8,128)} %param.7, f32[4]{0:T(128)S(1)} %get-tuple-element.28, f32[4]{0:T(128)S(1)} %get-tuple-element.27), kind=kLoop, calls=%fused_computation.3 | loop fusion | flops 2457600 | bytes 2457632 | tf_op jit(solution)/shard_map/convert_element_type | solution.py:575
  8.0 0.0 copy-done.1
  8.0 0.6 multiply_bitcast_fusion
  8.6 1.8 %reshape.169.mirrors_ref = bf16[640,640]{1,0:T(8,128)(2,1)} reshape(bf16[4,160,4,160]{3,2,1,0:T(4,128)(2,1)S(1)} %multiply_bitcast_fusion) | data formatting | bytes 1638400 | tf_op jit(solution)/shard_map/reshape | solution.py:555
  10.4 0.6 subtract_convert_fusion
  10.9 1.3 pad_maximum_fusion
  12.3 67.3 %one_step.1 = (f32[640,640]{1,0:T(8,128)}, bf16[640,640]{1,0:T(8,128)(2,1)}) custom-call(bf16[640,640]{1,0:T(8,128)(2,1)} %bitcast.25, bf16[5,2,128,640]{3,2,1,0:T(8,128)(2,1)} %bitcast.19, bf16[160,160]{1,0:T(8,128)(2,1)} %fusion.mirror_ref, bf16[640,640]{1,0:T(8,128)(2,1)} %reshape.169.mirrors_ref, f32[2,1,640]{2,1,0:T(1,128)} %tile.13.w_ref, ...), custom_call_target="tpu_custom_call" | custom-call | tf_op jit(solution)/shard_map/one_step/pallas_call | solution.py:466
  79.6 62.0 %last_step.1 = f32[640,640]{1,0:T(8,128)} custom-call(bf16[640,640]{1,0:T(8,128)(2,1)} %get-tuple-element.15.rates_ref, bf16[5,2,128,640]{3,2,1,0:T(8,128)(2,1)} %bitcast.20, bf16[160,160]{1,0:T(8,128)(2,1)} %fusion.mirror_ref, bf16[640,640]{1,0:T(8,128)(2,1)} %reshape.169.mirrors_ref, f32[2,1,640]{2,1,0:T(1,128)} %tile.13.w_ref, ...), custom_call_target="tpu_custom_call" | custom-call | tf_op jit(solution)/shard_map/last_step/pallas_call | solution.py:466
  141.5 2.7 %copy.18 = f32[4,160,640]{2,1,0:T(8,128)} copy(f32[4,160,640]{2,1,0:T(8,128)} %bitcast.22) | data formatting | bytes 3276800
  (18 shorter events, 0.2 us)
Async XLA Ops:
  0.0 0.9 copy-start
  0.9 7.1 %copy-start.1 = (f32[4,4]{1,0:T(4,128)}, f32[4,4]{1,0:T(4,128)S(1)}, u32[]{:S(2)}) copy-start(f32[4,4]{1,0:T(4,128)S(1)} %constant_dynamic-slice_fusion.4.par_ref) | copy-start | bytes 196

commit v2 on v1

--- a/solution.py
+++ b/solution.py
@@ -151,13 +151,9 @@
     )
 
 
-def step_kernel(nband, last, rates_ref, t_ref, mirror_ref, mirrors_ref, w_ref, b_hbm, a_ref, k_ref,
-                u_ref, drive_ref, par_ref, *rest):
-    if last:
-        un_ref, *rest = rest
-    else:
-        un_ref, rn_ref, *rest = rest
-    (face_ref, ps_ref, pr_ref, fz_ref, gz_ref, b_ref, own_ref, other_ref, x_ref, y_ref, s_ref, o_ref,
+def step_kernel(nband, t_ref, mirror_ref, mirrors_ref, w_ref, b_hbm, a_ref, k_ref,
+                u_ref, drive_ref, par_ref, un_ref, *rest):
+    (rates_ref, face_ref, ps_ref, pr_ref, fz_ref, gz_ref, b_ref, own_ref, other_ref, x_ref, y_ref, s_ref, o_ref,
      field_ref, pad_ref, edge_ref, around_ref, af_ref, col_ref, side_ref, we_ref,
      bsem, ps, pr, zs, zr, ss, rs, ys, yr, xs, xr, es, er) = rest
     band, lon = lax.axis_index("band"), lax.axis_index("lon")
@@ -235,11 +231,25 @@
     pl.semaphore_signal(barrier, inc=1, device_id=across, device_id_type=MESH)
     pl.semaphore_signal(barrier, inc=1, device_id=mate, device_id_type=MESH)
 
-    for i in range(npop):
-        part = pl.ds(i * nlat, nlat)
+    @pl.loop(0, npop)
+    def _(i):
+        gain, thresh = par_ref[0, i], par_ref[1, i]
+        for r in range(0, nlat, 16):
+            here = pl.ds(pl.multiple_of(i * nlat + r, 16), 16)
+            rates_ref[here] = jax.nn.sigmoid(gain * (u_ref[here] - thresh)).astype(rates_ref.dtype)
+        part = pl.ds(pl.multiple_of(i * nlat, 16), nlat)
         face_ref[part] = jnp.dot(
             mirror_ref[...], rates_ref[part], preferred_element_type=jnp.float32
         ).astype(face_ref.dtype)
+    pl.semaphore_wait(barrier, nband + 1)
+
+    @pl.loop(0, groups)
+    def _(g):
+        ps_ref[g] = lax.dot_general(
+            t_ref[g, 1], face_ref[...], along, preferred_element_type=jnp.float32
+        ).astype(ps_ref.dtype)
+        partial(g).start()
+
     fill = jnp.zeros((16 - npop, nlon), jnp.float32)
     for side, at in ((0, nlat - 1), (1, 0)):
         picked = [
@@ -253,15 +263,6 @@
         jnp.where(pick, 1.0, 0.0).astype(jnp.bfloat16), rates_ref[...], along,
         preferred_element_type=jnp.float32,
     ).astype(col_ref.dtype)
-    pl.semaphore_wait(barrier, nband + 1)
-
-    @pl.loop(0, groups)
-    def _(g):
-        ps_ref[g] = lax.dot_general(
-            t_ref[g, 1], face_ref[...], along, preferred_element_type=jnp.float32
-        ).astype(ps_ref.dtype)
-        partial(g).start()
-
     edge(0).start()
     edge(1).start()
     column().start()
@@ -404,7 +405,7 @@
 
     @pl.loop(0, npop)
     def _(i):
-        gain, thresh, decay, lateral = (par_ref[k, i] for k in range(4))
+        decay, lateral = par_ref[2, i], par_ref[3, i]
         base = pl.multiple_of(i * nlat, step)
         pad_ref[pl.ds(8, nlat)] = rates_ref[pl.ds(base, nlat)].astype(jnp.float32)
         pad_ref[7:8] = jnp.where(band > 0, af_ref[0, pl.ds(i, 1)], 0.0)
@@ -425,10 +426,7 @@
                 -decay * u + field_ref[here] * scale + lateral * beside
                 + drive_ref[here].astype(jnp.float32)
             )
-            u = u + time_step * forcing
-            un_ref[here] = u
-            if not last:
-                rn_ref[here] = jax.nn.sigmoid(gain * (u - thresh)).astype(rn_ref.dtype)
+            un_ref[here] = u + time_step * forcing
 
     edge(0).wait_send()
     edge(1).wait_send()
@@ -445,9 +443,9 @@
             cross(g, d).wait_send()
 
 
-def one_step(rates, table, mirror, mirrors, weights, basis, by_kind, kernels, u, drive, params,
+def one_step(table, mirror, mirrors, weights, basis, by_kind, kernels, u, drive, params,
              nband, npop, last):
-    rows, nlon = rates.shape
+    rows, nlon = u.shape
     owned, half_lat, deg = basis.shape
     nlat = rows // npop
     groups = table.shape[0]
@@ -457,18 +455,16 @@
     dma = pltpu.SemaphoreType.DMA
     vmem = pl.BlockSpec(memory_space=pltpu.VMEM)
     hbm = pl.BlockSpec(memory_space=pltpu.MemorySpace.HBM)
-    shapes = [jax.ShapeDtypeStruct(u.shape, jnp.float32)]
-    if not last:
-        shapes.append(jax.ShapeDtypeStruct(rates.shape, jnp.bfloat16))
     bf16 = jnp.bfloat16
     blocks = (groups, nband, 2 * group, rows)
     waves = nband * 2 * group
     return pl.pallas_call(
-        functools.partial(step_kernel, nband, last),
-        out_shape=tuple(shapes),
-        in_specs=[vmem] * 5 + [hbm] + [vmem] * 4 + [pl.BlockSpec(memory_space=pltpu.SMEM)],
-        out_specs=(vmem,) * len(shapes),
+        functools.partial(step_kernel, nband),
+        out_shape=jax.ShapeDtypeStruct(u.shape, jnp.float32),
+        in_specs=[vmem] * 4 + [hbm] + [vmem] * 4 + [pl.BlockSpec(memory_space=pltpu.SMEM)],
+        out_specs=vmem,
         scratch_shapes=[
+            pltpu.VMEM((rows, nlon), bf16),
             pltpu.VMEM((rows, nlon), bf16),
             pltpu.VMEM((groups, waves, rows), bf16),
             pltpu.VMEM((groups, waves, rows), bf16),
@@ -501,7 +497,7 @@
             collective_id=1 if last else 0, has_side_effects=True, vmem_limit_bytes=60 * 2**20
         ),
         name="last_step" if last else "one_step",
-    )(rates, table, mirror, mirrors, weights, basis, by_kind, kernels, u, drive, params)
+    )(table, mirror, mirrors, weights, basis, by_kind, kernels, u, drive, params)
 
 
 def wave_table(starts, owned, longitude, period):
@@ -531,7 +527,6 @@
     band, lon, pop = lax.axis_index("band"), lax.axis_index("lon"), lax.axis_index("pop")
     pop_first = pop * npop
     params = lax.dynamic_slice_in_dim(rate_params, pop_first, npop, 1)
-    gain_row, thresh = params[0, :, None, None], params[1, :, None, None]
 
     bands = jnp.arange(nband, dtype=jnp.int32)
     kk = jnp.arange(nlon, dtype=jnp.int32)
@@ -550,9 +545,9 @@
     south = band >= hb
     lat = jnp.arange(nlat, dtype=jnp.int32)
     mirror = (lat[:, None] == jnp.where(south, nlat - 1 - lat, lat)[None, :]).astype(jnp.bfloat16)
-    back = (lat[:, None] == nlat - 1 - lat[None, :]).astype(jnp.bfloat16)
-    mirrors = jnp.einsum("xy,ab->xayb", jnp.eye(npop, dtype=jnp.bfloat16), back)
-    mirrors = mirrors.reshape(rows, rows)
+    cell = jnp.arange(rows, dtype=jnp.int32)
+    image = cell // nlat * nlat + (nlat - 1 - cell % nlat)
+    mirrors = (cell[:, None] == image[None, :]).astype(jnp.bfloat16)
 
     coup_own = lax.dynamic_slice_in_dim(coupling, pop_first, npop, 0)
     block_own = lax.dynamic_slice_in_dim(conn_block, pop_first, npop, 0)
@@ -572,18 +567,11 @@
 
     drive = drive.reshape(rows, nlon)
     u = activity.reshape(rows, nlon)
-    rates = jax.nn.sigmoid(gain_row * (activity - thresh)).astype(jnp.bfloat16)
-    rates = rates.reshape(rows, nlon)
     for step_index in range(STEPS):
-        last = step_index == STEPS - 1
-        results = one_step(
-            rates, table, mirror, mirrors, weights, basis, by_kind, kernels, u, drive, params,
-            nband, npop, last,
-        )
-        if last:
-            (u,) = results
-        else:
-            u, rates = results
+        u = one_step(
+            table, mirror, mirrors, weights, basis, by_kind, kernels, u, drive, params,
+            nband, npop, step_index == STEPS - 1,
+        )
     return u.reshape(npop, nlat, nlon)
 
 

time: 144 us -> 140 us (0.972)
  other arithmetic: 7.73 us -> 5.45 us
    reshape x1 -> x0, local copies, waits for them, and re-layouts: 1.76 us -> none  [fast_local(): mirrors = mirrors.reshape(rows, rows)]
    convert_element_type x1, other arithmetic: 2.86 us -> 1.16 us  [fast_local(): mirrors = (cell[:, None] == image[None, :]).astype(jnp.bfloat16)]
where the time goes in v2:
time: 140 us; the launch traced here: 139 us
  Pallas kernels  128 us (91%)
  local copies, waits for them, and re-layouts  5.95 us (4%)
  other arithmetic  5.45 us (4%)
    pallas_call x2, Pallas kernels, one_step(): pl.pallas_call(functools.partial(step_kernel, nband), out_shape=jax.Shape...  128 us

profile of v2, /device:TPU:0, one launch (start us, length us, event | category | flops | bytes accessed | tf_op | source)
XLA Modules:
  0.0 139.4 jit_solution(10189682970528641490)
XLA Ops:
  0.0 0.0 copy-start
  0.0 0.1 pad_add_fusion
  0.1 1.3 constant_dynamic-slice_fusion.par_ref
  1.4 0.0 copy-done
  1.4 0.1 copy.12
  1.5 0.7 constant_dynamic-slice_fusion.3
  2.2 0.1 copy.13
  2.3 0.1 sine_multiply_fusion
  2.4 0.1 broadcast_add_fusion
  2.5 0.7 tile.13.w_ref
  3.2 0.7 fusion.1.mirror_ref
  3.8 0.2 fusion.13
  4.0 0.1 broadcast_multiply_fusion
  4.1 0.2 mul.223
  4.3 0.1 copy.15
  4.4 0.1 copy.14
  4.4 0.7 pad_maximum_fusion.2.a_ref
  5.1 0.5 fusion.6
  5.7 1.2 fusion.mirrors_ref
  6.9 0.6 subtract_convert_fusion
  7.4 1.3 pad_maximum_fusion
  8.8 66.1 %one_step.1.u_ref = f32[640,640]{1,0:T(8,128)} custom-call(bf16[5,2,128,640]{3,2,1,0:T(8,128)(2,1)} %bitcast.12, bf16[160,160]{1,0:T(8,128)(2,1)} %fusion.1.mirror_ref, bf16[640,640]{1,0:T(8,128)(2,1)} %fusion.mirrors_ref, f32[2,1,640]{2,1,0:T(1,128)} %tile.13.w_ref, bf16[80,320,640]{2,1,0:T(8,128)(2,1)} %b_hbm.3, bf16[32,32]{1,0:T(8,128)(2,1)} %pad_maximum_fusion.2.a_ref, ...), custom_call_target="tpu_custom_call" | custom-call | tf_op jit(solution)/shard_map/one_step/pallas_call | solution.py:461
  74.9 61.8 %last_step.1 = f32[640,640]{1,0:T(8,128)} custom-call(bf16[5,2,128,640]{3,2,1,0:T(8,128)(2,1)} %bitcast.13, bf16[160,160]{1,0:T(8,128)(2,1)} %fusion.1.mirror_ref, bf16[640,640]{1,0:T(8,128)(2,1)} %fusion.mirrors_ref, f32[2,1,640]{2,1,0:T(1,128)} %tile.13.w_ref, bf16[80,320,640]{2,1,0:T(8,128)(2,1)} %b_hbm.3, bf16[32,32]{1,0:T(8,128)(2,1)} %pad_maximum_fusion.2.a_ref, ...), custom_call_target="tpu_custom_call" | custom-call | tf_op jit(solution)/shard_map/last_step/pallas_call | solution.py:461
  136.7 2.7 %copy.18 = f32[4,160,640]{2,1,0:T(8,128)} copy(f32[4,160,640]{2,1,0:T(8,128)} %bitcast.14) | data formatting | bytes 3276800
  (15 shorter events, 0.1 us)
Async XLA Ops:
  0.0 1.4 %copy-start = (s32[8,8]{1,0:T(8,128)S(1)}, s32[8,8]{1,0:T(8,128)}, u32[]{:S(2)}) copy-start(s32[8,8]{1,0:T(8,128)} %param.11) | copy-start | bytes 772

commit v3 on v2

--- a/solution.py
+++ b/solution.py
@@ -305,7 +305,7 @@
             x = jnp.concatenate(x, axis=1)[:, :half_lat].astype(jnp.bfloat16)
             parity = jnp.dot(x, b_ref[m], preferred_element_type=jnp.float32)
             gap = degree - (first + m)
-            coeffs = jnp.where(gap % 2 == 0, parity[:half], parity[half:])
+            coeffs = jnp.where((gap & 1) == 0, parity[:half], parity[half:])
             own_ref[m] = jnp.where(gap >= 0, coeffs, 0.0).astype(own_ref.dtype)
         swap(g).start()
 
@@ -324,7 +324,7 @@
             for kind in range(1, kinds):
                 mixed += k_ref[kind : kind + 1] * by_kind[kind * half : (kind + 1) * half]
             gap = degree - (first + m)
-            signed = jnp.where(gap % 2 == 0, mixed, -mixed)
+            signed = jnp.where((gap & 1) == 0, mixed, -mixed)
             y = lax.dot_general(
                 jnp.concatenate([mixed, signed], axis=0).astype(jnp.bfloat16), b_ref[m],
                 along, preferred_element_type=jnp.float32,

time: 140 us -> 140 us (level)
  no operation moved by 1% of the time
where the time goes in v3:
time: 140 us; the launch traced here: 139 us
  Pallas kernels  128 us (91%)
  local copies, waits for them, and re-layouts  5.95 us (4%)
  other arithmetic  5.45 us (4%)
    pallas_call x2, Pallas kernels, one_step(): pl.pallas_call(functools.partial(step_kernel, nband), out_shape=jax.Shape...  128 us

profile of v3, /device:TPU:0, one launch (start us, length us, event | category | flops | bytes accessed | tf_op | source)
XLA Modules:
  0.0 139.4 jit_solution(6920728214360084890)
XLA Ops:
  0.0 0.0 copy-start
  0.0 0.1 pad_add_fusion
  0.1 1.3 constant_dynamic-slice_fusion.par_ref
  1.4 0.0 copy-done
  1.4 0.1 copy.12
  1.5 0.7 constant_dynamic-slice_fusion.3
  2.2 0.1 copy.13
  2.3 0.1 sine_multiply_fusion
  2.4 0.1 broadcast_add_fusion
  2.5 0.7 tile.13.w_ref
  3.2 0.7 fusion.1.mirror_ref
  3.8 0.2 fusion.13
  4.0 0.1 broadcast_multiply_fusion
  4.1 0.2 mul.223
  4.3 0.1 copy.15
  4.4 0.1 copy.14
  4.4 0.7 pad_maximum_fusion.2.a_ref
  5.1 0.5 fusion.6
  5.7 1.2 fusion.mirrors_ref
  6.9 0.6 subtract_convert_fusion
  7.4 1.3 pad_maximum_fusion
  8.8 66.1 %one_step.1.u_ref = f32[640,640]{1,0:T(8,128)} custom-call(bf16[5,2,128,640]{3,2,1,0:T(8,128)(2,1)} %bitcast.12, bf16[160,160]{1,0:T(8,128)(2,1)} %fusion.1.mirror_ref, bf16[640,640]{1,0:T(8,128)(2,1)} %fusion.mirrors_ref, f32[2,1,640]{2,1,0:T(1,128)} %tile.13.w_ref, bf16[80,320,640]{2,1,0:T(8,128)(2,1)} %b_hbm.3, bf16[32,32]{1,0:T(8,128)(2,1)} %pad_maximum_fusion.2.a_ref, ...), custom_call_target="tpu_custom_call" | custom-call | tf_op jit(solution)/shard_map/one_step/pallas_call | solution.py:461
  74.9 61.8 %last_step.1 = f32[640,640]{1,0:T(8,128)} custom-call(bf16[5,2,128,640]{3,2,1,0:T(8,128)(2,1)} %bitcast.13, bf16[160,160]{1,0:T(8,128)(2,1)} %fusion.1.mirror_ref, bf16[640,640]{1,0:T(8,128)(2,1)} %fusion.mirrors_ref, f32[2,1,640]{2,1,0:T(1,128)} %tile.13.w_ref, bf16[80,320,640]{2,1,0:T(8,128)(2,1)} %b_hbm.3, bf16[32,32]{1,0:T(8,128)(2,1)} %pad_maximum_fusion.2.a_ref, ...), custom_call_target="tpu_custom_call" | custom-call | tf_op jit(solution)/shard_map/last_step/pallas_call | solution.py:461
  136.7 2.7 %copy.18 = f32[4,160,640]{2,1,0:T(8,128)} copy(f32[4,160,640]{2,1,0:T(8,128)} %bitcast.14) | data formatting | bytes 3276800
  (15 shorter events, 0.1 us)
Async XLA Ops:
  0.0 1.4 %copy-start = (s32[8,8]{1,0:T(8,128)S(1)}, s32[8,8]{1,0:T(8,128)}, u32[]{:S(2)}) copy-start(s32[8,8]{1,0:T(8,128)} %param.11) | copy-start | bytes 772
